TPU v7x, 32 devices: a whole 2x2x4 slice. The times are simulated.
32 devices in a mesh: groups: 2 (over y), seq: 16 (over z, x, core).
Axes of the slice: x: 2, y: 2, z: 4, core: 2. Of those that a mesh axis runs over, the one named last changes fastest.
Arguments:
- pool_kv: bfloat16 [3072, 1024], P(('groups', 'seq')), parts along dimension 0, may hold values from -6 to 6
- pool_slot: int32 [32], P('groups'), parts along dimension 0, may hold values from 0 to 15, each once
- passage_order: int32 [32], P('groups'), parts along dimension 0, may hold values from 0 to 15, each once
- passage_start: int32 [32], P('groups'), parts along dimension 0, may hold values from 0 to 6784, as said below
- recompute_pos: int32 [32, 56], P('groups'), parts along dimension 0, may hold values from 0 to 383, as said below
- page_table: int32 [3072], P('groups'), parts along dimension 0, may hold values from 0 to 1535, as said below
- fresh_q: bfloat16 [1792, 1024], P(('groups', 'seq')), parts along dimension 0, may hold values from -64 to 64
- fresh_kv: bfloat16 [1792, 256], P(('groups', 'seq')), parts along dimension 0, may hold values from -64 to 64
Outputs:
- attended: bfloat16 [1792, 1024], P(('groups', 'seq')), parts along dimension 0
- decode_cache: bfloat16 [3072, 1024], P(('groups', 'seq')), parts along dimension 0
There are 2 independent parts, one for each index of `groups`. A program takes and returns all parts, laid end to end along the dimension named above; each array names one. Nothing has to cross between parts.
Inputs may be any that keep to these rules, and one draw needn't show every extreme that they name: `passage_start`: increases by at least 384 from one passage to the next; the first is 0 and the last is (15) * 384 + 1024. `recompute_pos`: each row holds 56 different positions of its passage in increasing order. `page_table`: every row of the decode cache receives exactly one page; of the 96 pages of one passage at most 6 go to the 96 rows of one owner, and that many do for some owner.
All inputs are finite; a program needn't handle non-finite values.
Results may differ from a plain program's by a relative error of at most 0.0075.
The roundings to bfloat16 on the way count: a program that leaves them out, or rounds other values in their place, can miss the bound.
Values may be sent and summed in bfloat16 or wider, within the bound.
A program may use at most 256 MiB of HBM per device.

v0:
```python
import jax
import jax.numpy as jnp
from jax import lax
from jax.experimental import pallas as pl
from jax.experimental.pallas import tpu as pltpu
from jax.sharding import PartitionSpec as P

GROUP = 8
PAGE = 4


ROPE_BASE = 500000.0
LOG2_E = 1.4426950408889634


def rotate_pos(vector, positions):
    half_dim = vector.shape[-1] // 2
    frequency = ROPE_BASE ** (-(jnp.arange(half_dim, dtype=jnp.float32) * (2.0 / vector.shape[-1])))
    angles = positions.astype(jnp.float32)[..., None] * frequency
    cosine = jnp.cos(angles)
    sine = jnp.sin(angles)
    lower_half = vector[..., :half_dim]
    upper_half = vector[..., half_dim:]
    return jnp.concatenate(
        [lower_half * cosine - upper_half * sine, upper_half * cosine + lower_half * sine], axis=-1
    )


MESH = pl.DeviceIdType.MESH


PIECES = 3


def piece_rows(rows, count):
    halves = max(2, 2 * (count // 4 - 1))
    cut = rows * (halves - 1) // halves // 16 * 16
    size = -(-cut // (PIECES * 16)) * 16
    return [(at, min(size, cut - at)) for at in range(0, cut, size)] + [(cut, rows - cut)]


def spread_kernel(count, block_ref, all_ref, send_sem, recv_sem, own_sem):
    rows = block_ref.shape[0]
    length = count // 4
    parts = [pl.ds(*piece) for piece in piece_rows(rows, count)]
    last = len(parts) - 1
    lined = range(last)
    me = lax.axis_index("seq")
    at = me // 4
    inner = lax.rem(me, 4)
    core = lax.rem(inner, 2)
    across_inner = lax.rem(inner + 2, 4)
    across = at * 4 + across_inner
    sibling = me + 1 - 2 * core
    twin_inner = inner + 1 - 2 * core
    up, down = me + 4, me - 4
    has_up, has_down = at < length - 1, at > 0

    barrier = pltpu.get_barrier_semaphore()

    def greet(device):
        pl.semaphore_signal(barrier, inc=1, device_id={"seq": device}, device_id_type=MESH)

    greet(across)
    greet(sibling)
    pl.when(has_up)(lambda: greet(up))
    pl.when(has_down)(lambda: greet(down))
    pl.semaphore_wait(barrier, 2 + jnp.where(has_up, 1, 0) + jnp.where(has_down, 1, 0))

    def copy(part, block, way, device, own=False):
        source = block_ref.at[parts[part]] if own else all_ref.at[block, parts[part]]
        return pltpu.make_async_remote_copy(
            src_ref=source,
            dst_ref=all_ref.at[block, parts[part]],
            send_sem=send_sem.at[way, part, block],
            recv_sem=recv_sem.at[part, block],
            device_id={"seq": device},
            device_id_type=MESH,
        )

    def begin(part, block, way, device, own=False):
        copy(part, block, way, device, own).start()

    def arrive(part, block):
        copy(part, block, 0, sibling).wait_recv()

    local = pltpu.make_async_copy(block_ref, all_ref.at[me], own_sem)
    local.start()

    def send_own(act):
        act(last, me, 2, across, True)
        for part in lined:
            pl.when(has_up)(lambda part=part: act(part, me, 0, up, True))
            pl.when(has_down)(lambda part=part: act(part, me, 1, down, True))
        pl.when(has_up)(lambda: act(last, me, 0, up, True))
        pl.when(has_down)(lambda: act(last, me, 1, down, True))
        for part in lined:
            act(part, me, 2, across, True)
        for part in (last, *lined):
            act(part, me, 3, sibling, True)

    def pass_across_first(act):
        pl.when(has_up)(lambda: act(last, across, 0, up))
        pl.when(has_down)(lambda: act(last, across, 1, down))
        act(last, across, 3, sibling)

    def each(step, act, wait):
        for part, where, cross in (
            *((part, inner, True) for part in lined),
            (last, inner, False),
            (last, across_inner, False),
        ):
            for way, exists, more, device, place in (
                (0, at - step >= 0, has_up, up, at - step),
                (1, at + step < length, has_down, down, at + step),
            ):
                block = place * 4 + where

                @pl.when(exists)
                def _(part=part, block=block, cross=cross, way=way, more=more, device=device):
                    if wait:
                        arrive(part, block)
                    pl.when(more)(lambda: act(part, block, way, device))
                    if cross:
                        act(part, block, 2, across)
                    act(part, block, 3, sibling)

    def crossed(step, act, wait):
        for exists, place in ((at - step >= 0, at - step), (at + step < length, at + step)):

            @pl.when(exists)
            def _(place=place):
                block = place * 4 + across_inner
                for part in lined:
                    if wait:
                        arrive(part, block)
                    act(part, block, 3, sibling)

    def crossed_here(act, wait):
        for part in lined:
            if wait:
                arrive(part, across)
            act(part, across, 3, sibling)

    send_own(begin)
    arrive(last, across)
    pass_across_first(begin)

    @pl.loop(1, length)
    def _(step):
        each(step, begin, True)
        pl.when(step == 1)(lambda: crossed_here(begin, True))
        pl.when(step > 1)(lambda: crossed(step - 1, begin, True))

    if length == 1:
        crossed_here(begin, True)
    else:
        crossed(length - 1, begin, True)

    @pl.loop(0, length)
    def _(place):
        for other in range(2):
            block = place * 4 + other * 2 + lax.rem(core + 1, 2)
            for part in range(last + 1):
                arrive(part, block)

    def settle(part, block, way, device, own=False):
        copy(part, block, way, device, own).wait_send()

    send_own(settle)
    pass_across_first(settle)

    @pl.loop(1, length)
    def _(step):
        each(step, settle, False)
        crossed(step, settle, False)

    crossed_here(settle, False)
    local.wait()


def spread(block, count):
    rows, width = block.shape
    return pl.pallas_call(
        lambda *refs: spread_kernel(count, *refs),
        out_shape=jax.ShapeDtypeStruct((count, rows, width), block.dtype),
        in_specs=[pl.BlockSpec(memory_space=pltpu.VMEM)],
        out_specs=pl.BlockSpec(memory_space=pl.ANY),
        scratch_shapes=[
            pltpu.SemaphoreType.DMA((4, len(piece_rows(rows, count)), count)),
            pltpu.SemaphoreType.DMA((len(piece_rows(rows, count)), count)),
            pltpu.SemaphoreType.DMA,
        ],
        compiler_params=pltpu.CompilerParams(collective_id=0, has_side_effects=True),
    )(block)


def blend_kernel(
    all_ref, turn_ref, key_pos_ref, query_ref, query_pos_ref, token_ref,
    attended_ref, pages_ref, peak_ref, sum_ref, mixed_ref, page_key_ref, page_value_ref,
):
    step = pl.program_id(0)
    together, unit, width = all_ref.shape
    head_dim = width // 2
    half_dim = head_dim // 2
    count = together * unit

    @pl.when(step == 0)
    def _():
        peak_ref[...] = jnp.full(peak_ref.shape, -1e30, jnp.float32)
        sum_ref[...] = jnp.zeros(sum_ref.shape, jnp.float32)
        mixed_ref[...] = jnp.zeros(mixed_ref.shape, jnp.float32)
        page_key_ref[...] = jnp.zeros(page_key_ref.shape, jnp.float32)
        page_value_ref[...] = jnp.zeros(page_value_ref.shape, jnp.float32)

    rows = all_ref[...].reshape(count, width)
    raw = rows[:, :head_dim].astype(jnp.float32)
    values = rows[:, head_dim:]
    pages = turn_ref.shape[1]
    owner = lax.broadcasted_iota(jnp.int32, (unit, pages), 0) // PAGE
    expand = jnp.where(
        owner == lax.broadcasted_iota(jnp.int32, (unit, pages), 1), 1.0, 0.0
    ).astype(jnp.bfloat16)

    def unfold(table):
        high = table.astype(jnp.bfloat16)
        rest = table - high.astype(jnp.float32)
        middle = rest.astype(jnp.bfloat16)
        low = (rest - middle.astype(jnp.float32)).astype(jnp.bfloat16)
        thirds = jnp.dot(
            expand,
            jnp.concatenate([high, middle, low], axis=1),
            preferred_element_type=jnp.float32,
        )
        return (
            thirds[:, :head_dim]
            + thirds[:, head_dim : 2 * head_dim]
            + thirds[:, 2 * head_dim :]
        )

    at_row = lax.broadcasted_iota(jnp.int32, (unit, head_dim), 0)
    at_lane = lax.broadcasted_iota(jnp.int32, (unit, head_dim), 1)
    still = jnp.where((at_row >= pages * PAGE) & (at_lane < half_dim), 1.0, 0.0)
    turn = jnp.concatenate(
        [
            unfold(turn_ref[part])
            + still
            for part in range(together)
        ],
        axis=0,
    )
    turned = pltpu.roll(turn, half_dim, 1)
    first = lax.broadcasted_iota(jnp.int32, (count, head_dim), 1) < half_dim
    cosine = jnp.where(first, turn, turned)
    sine = jnp.where(first, -turned, turn)
    keys = (raw * cosine + pltpu.roll(raw, half_dim, 1) * sine).astype(jnp.bfloat16)

    scores = lax.dot_general(
        query_ref[...], keys, (((1,), (1,)), ((), ())), preferred_element_type=jnp.float32
    )
    slope = head_dim ** (-0.5) * LOG2_E
    scores = jnp.where(key_pos_ref[0] <= query_pos_ref[...], scores, -1e30)
    old_peak = peak_ref[...]
    peak = jnp.maximum(old_peak, jnp.max(scores, axis=1, keepdims=True))
    shrink = jnp.exp2((old_peak - peak) * slope)
    weights = jnp.exp2((scores - peak) * slope)
    peak_ref[...] = peak
    sum_ref[...] = sum_ref[...] * shrink + jnp.sum(weights, axis=1, keepdims=True)
    mixed_ref[...] = mixed_ref[...] * shrink + jnp.dot(
        weights.astype(jnp.bfloat16), values, preferred_element_type=jnp.float32
    )

    local = token_ref[...] - step * count
    lanes = lax.broadcasted_iota(jnp.int32, (token_ref.shape[0], count), 1)
    choose = jnp.where(lanes == local, 1.0, 0.0).astype(jnp.bfloat16)
    page_key_ref[...] += jnp.dot(choose, keys, preferred_element_type=jnp.float32)
    page_value_ref[...] += jnp.dot(choose, values, preferred_element_type=jnp.float32)

    @pl.when(step == pl.num_programs(0) - 1)
    def _():
        mixed_ref[...] = mixed_ref[...] / sum_ref[...]
        for head in range(GROUP):
            attended_ref[:, head * head_dim : (head + 1) * head_dim] = mixed_ref[
                pl.ds(head, attended_ref.shape[0], stride=GROUP), :
            ].astype(jnp.bfloat16)
        for token in range(PAGE):
            for at, held in enumerate((page_key_ref, page_value_ref)):
                start = (2 * token + at) * head_dim
                pages_ref[:, start : start + head_dim] = held[
                    pl.ds(token, pages_ref.shape[0], stride=PAGE), :
                ].astype(jnp.bfloat16)


def blend(everything, turn, key_pos, queries, query_pos, tokens):
    count, unit, width = everything.shape
    head_dim = width // 2
    together = 4
    steps = count // together
    query_count = queries.shape[0]
    token_count = tokens.shape[0]

    def whole(shape):
        return pl.BlockSpec(shape, lambda i: (0, 0))

    return pl.pallas_call(
        blend_kernel,
        grid=(steps,),
        out_shape=(
            jax.ShapeDtypeStruct((query_count // GROUP, GROUP * head_dim), jnp.bfloat16),
            jax.ShapeDtypeStruct((token_count // PAGE, PAGE * width), jnp.bfloat16),
        ),
        in_specs=[
            pl.BlockSpec((together, unit, width), lambda i: (i, 0, 0)),
            pl.BlockSpec((together, token_count // PAGE, head_dim), lambda i: (i, 0, 0)),
            pl.BlockSpec((1, 1, together * unit), lambda i: (i, 0, 0)),
            whole((query_count, head_dim)),
            whole((query_count, 1)),
            whole((token_count, 1)),
        ],
        out_specs=(
            whole((query_count // GROUP, GROUP * head_dim)),
            whole((token_count // PAGE, PAGE * width)),
        ),
        scratch_shapes=[
            pltpu.VMEM((query_count, 1), jnp.float32),
            pltpu.VMEM((query_count, 1), jnp.float32),
            pltpu.VMEM((query_count, head_dim), jnp.float32),
            pltpu.VMEM((token_count, head_dim), jnp.float32),
            pltpu.VMEM((token_count, head_dim), jnp.float32),
        ],
    )(
        everything,
        turn,
        key_pos.reshape(steps, 1, together * unit),
        queries,
        query_pos[:, None],
        tokens[:, None],
    )


def pick(one_hot, table):
    return jnp.dot(one_hot.astype(jnp.float32), table, precision=lax.Precision.HIGHEST)


def shards(
    pool_kv, pool_slot, passage_order, passage_start, recompute_pos, page_table, fresh_q, fresh_kv
):
    seq_count = lax.axis_size("seq")
    my_index = lax.axis_index("seq")
    page_count = pool_kv.shape[0]
    head_dim = fresh_kv.shape[1] // 2
    half_dim = head_dim // 2
    sel_count = fresh_q.shape[0]
    tok_count = page_count * PAGE
    total_pages = seq_count * page_count
    bf16 = jnp.bfloat16

    filled = tok_count + sel_count
    unit = -(-filled // 64) * 64
    far = jnp.int32(2**30)

    passage_ids = jnp.arange(seq_count, dtype=jnp.int32)
    mine = (passage_ids == my_index)[:, None]
    picked = jnp.sum(jnp.where(mine, recompute_pos, 0), axis=0)
    start_pos = jnp.sum(jnp.where(mine[:, 0], passage_start, 0))
    fresh_pos = start_pos + picked
    fresh_keys = rotate_pos(fresh_kv[:, :head_dim].astype(jnp.float32), fresh_pos).astype(bf16)
    block = jnp.concatenate(
        [
            pool_kv.reshape(tok_count, 2 * head_dim),
            jnp.concatenate([fresh_keys, fresh_kv[:, head_dim:]], axis=1),
            jnp.zeros((unit - filled, 2 * head_dim), bf16),
        ],
        axis=0,
    )
    everything = spread(block, seq_count)

    placed = passage_order[:, None] == passage_ids[None, :]
    slots = jnp.sum(jnp.where(placed, pool_slot[None, :], 0), axis=1)

    frequency = ROPE_BASE ** (-(jnp.arange(half_dim, dtype=jnp.float32) * (2.0 / head_dim)))
    start_angles = passage_start.astype(jnp.float32)[:, None] * frequency
    start_table = jnp.concatenate([jnp.cos(start_angles), jnp.sin(start_angles)], axis=1)
    recompute_rows = recompute_pos.astype(jnp.float32)

    row_ids = jnp.arange(total_pages, dtype=jnp.int32)
    spot = (row_ids % page_count) * seq_count + row_ids // page_count
    row_slot = spot // page_count
    row_page = spot % page_count
    row_hot = row_slot[:, None] == slots[None, :]
    row_passage = jnp.sum(jnp.where(row_hot, passage_ids[None, :], 0), axis=1)
    row_turn = pick(row_hot, start_table)
    row_recompute = pick(row_hot, recompute_rows)
    lane = jnp.arange(PAGE, dtype=jnp.int32)
    row_tok = row_page[:, None] * PAGE + lane[None, :]
    replaced = jnp.any(
        row_recompute[:, None, :] == row_tok[:, :, None].astype(jnp.float32), axis=2
    )
    cached_pos = jnp.where(replaced, far, row_passage[:, None] * tok_count + row_tok).reshape(-1)
    fresh_place = passage_ids[:, None] * tok_count + recompute_pos
    key_pos = jnp.concatenate(
        [
            cached_pos.reshape(seq_count, tok_count),
            fresh_place,
            jnp.full((seq_count, unit - filled), far, jnp.int32),
        ],
        axis=1,
    )
    turn = row_turn.reshape(seq_count, page_count, head_dim)

    my_rows = my_index * page_count + jnp.arange(page_count, dtype=jnp.int32)
    source = jnp.sum(
        jnp.where(
            page_table[None, :] == my_rows[:, None],
            jnp.arange(total_pages, dtype=jnp.int32)[None, :],
            0,
        ),
        axis=1,
    )
    source_passage = source // page_count
    source_page = source % page_count
    source_hot = source_passage[:, None] == passage_ids[None, :]
    source_spot = (
        jnp.sum(jnp.where(source_hot, slots[None, :], 0), axis=1) * page_count + source_page
    )
    source_row = (source_spot % seq_count) * unit + source_spot // seq_count * PAGE
    source_recompute = pick(source_hot, recompute_rows)
    source_tok = source_page[:, None] * PAGE + lane[None, :]
    match = source_recompute[:, None, :] == source_tok[:, :, None].astype(jnp.float32)
    sel_ids = jnp.arange(sel_count, dtype=jnp.int32)
    sel_at = jnp.sum(jnp.where(match, sel_ids[None, None, :] + 1, 0), axis=2)
    token_at = jnp.where(
        sel_at > 0,
        source_passage[:, None] * unit + tok_count + sel_at - 1,
        source_row[:, None] + lane[None, :],
    ).reshape(-1)
    queries = rotate_pos(
        fresh_q.reshape(sel_count, GROUP, head_dim).astype(jnp.float32), fresh_pos[:, None]
    ).astype(bf16)
    query_rows = queries.reshape(-1, head_dim)
    query_pos = jnp.repeat(my_index * tok_count + picked, GROUP)
    attended, pages = blend(everything, turn, key_pos, query_rows, query_pos, token_at)
    return (attended, pages)


def solution(mesh):
    placed = (
        P(("groups", "seq"), None),
        P("groups"),
        P("groups"),
        P("groups"),
        P("groups", None),
        P("groups"),
        P(("groups", "seq"), None),
        P(("groups", "seq"), None),
    )
    return jax.shard_map(
        shards,
        mesh=mesh,
        in_specs=placed,
        out_specs=(P(("groups", "seq"), None), P(("groups", "seq"), None)),
        check_vma=False,
    )
```

profile of v0, /device:TPU:0, one launch (start us, length us, event | category | flops | bytes accessed | tf_op | source)
XLA Modules:
  0.0 61.6 jit_solution(10457366061192565952)
XLA Ops:
  0.7 1.0 %select_reduce_fusion = s32[96]{0:T(128)S(1)} fusion(s32[1536]{0:T(1024)} %param.13, s32[96]{0:T(128)S(1)} %iota_add_fusion.1), kind=kLoop, calls=%fused_computation.1 | loop fusion | flops 442272 | bytes 6912 | tf_op jit(solution)/shard_map/reduce_sum | solution.py:412
  1.6 0.9 %select_reduce_fusion.3 = s32[16]{0:T(128)S(1)} fusion(s32[16]{0:T(128)} %param.9, s32[16]{0:T(128)} %param.10), kind=kLoop, calls=%fused_computation.68 | loop fusion | flops 752 | bytes 192 | tf_op jit(solution)/shard_map/reduce_sum | solution.py:379
  2.6 1.4 %fusion.41 = (f32[16]{0:T(128)S(1)}, s32[]{:T(128)}) fusion(s32[16]{0:T(128)} %param.11, s32[]{:T(128)S(6)} %axis_index.12), kind=kLoop, calls=%fused_computation.99 | loop fusion | flops 63 | bytes 136 | tf_op jit(solution)/shard_map/convert_element_type | solution.py:382
  4.0 0.1 select_reduce_fusion.2
  4.2 0.8 %broadcast_add_fusion = (s32[16,56]{1,0:T(8,128)S(1)}, s32[56]{0:T(128)S(1)}) fusion(s32[16,56]{1,0:T(8,128)} %param.12, s32[16]{0:T(128)S(1)} %iota_multiply_fusion, pred[16]{0:T(512)(128)(4,1)S(1)} %iota_compare_fusion.3), kind=kLoop, calls=%fused_computation.75 | loop fusion | flops 2632 | bytes 7472 | tf_op jit(solution)/shard_map/add | solution.py:400
  5.0 0.6 %broadcast_add_fusion.1 = (s32[56]{0:T(128)S(1)}, f32[56]{0:T(128)S(1)}) fusion(s32[56]{0:T(128)S(1)} %get-tuple-element.11, s32[]{:T(128)S(6)} %mul.235, s32[]{:T(128)} %get-tuple-element.23), kind=kLoop, calls=%fused_computation.97 | loop fusion | flops 168 | bytes 680 | tf_op jit(solution)/shard_map/add | solution.py:441
  5.7 0.1 fusion.6
  5.9 0.1 multiply_cosine_fusion.1
  6.1 0.9 %fusion.33 = f32[96,56]{0,1:T(8,128)S(1)} fusion(s32[16,56]{1,0:T(8,128)} %param.12, s32[96]{0:T(128)S(1)} %get-tuple-element.3), kind=kOutput, calls=%fused_computation.65 | convolution fusion | flops 1034624 | bytes 25472 | tf_op jit(solution)/shard_map/dot_general | solution.py:342
  7.0 0.1 select_reduce_fusion.1
  7.1 0.1 copy.26
  7.2 0.8 %slice_convert_fusion = (f32[56,128]{1,0:T(8,128)S(1)}, bf16[56,128]{1,0:T(8,128)(2,1)S(1)}) fusion(bf16[56,256]{1,0:T(8,128)(2,1)} %param.15), kind=kLoop, calls=%fused_computation.48 | loop fusion | flops 7168 | bytes 71680 | tf_op jit(solution)/shard_map/convert_element_type | solution.py:367
  8.0 0.1 copy.29
  8.1 0.1 fusion.10
  8.2 0.1 add.297
  8.3 0.2 multiply_cosine_fusion
  8.5 0.1 copy.27
  8.6 0.8 %select_n.162.token_ref = s32[384,1]{1,0:T(8,128)} reshape(s32[96,4]{1,0:T(8,128)S(1)} %copy.29) | data formatting | bytes 3072 | tf_op jit(solution)/shard_map/jit(_where)/select_n | solution.py:432
  9.5 0.1 copy.28
  9.6 0.1 reshape.344
  9.7 0.8 %maximum_maximum_fusion.refs_0_ = bf16[448,256]{1,0:T(8,128)(2,1)} fusion(bf16[56,128]{1,0:T(8,128)(2,1)S(1)} %get-tuple-element.9, bf16[56,64]{1,0:T(8,128)(2,1)S(1)} %get-tuple-element.14, bf16[56,64]{1,0:T(8,128)(2,1)S(1)} %get-tuple-element.15, bf16[384,256]{1,0:T(8,128)(2,1)S(1)} %reshape.344, bf16[448]{0:T(512)(128)(2,1)S(1)} %pad.11.clone), kind=kLoop, calls=%fused_computation.2 | loop fusion | flops 1146880 | bytes 455552 | tf_op jit(solution)/shard_map/concatenate | solution.py:368
  10.5 0.8 %broadcast_in_dim_reshape.5.query_pos_ref = s32[448,1]{1,0:T(8,128)} reshape(s32[56,8]{1,0:T(8,128)S(1)} %broadcast_in_dim.133) | data formatting | bytes 3584 | tf_op jit(solution)/shard_map/broadcast_in_dim;reshape | solution.py:336
  11.4 0.1 fusion.4
  11.6 0.8 %pad_maximum_fusion.query_ref = bf16[448,128]{1,0:T(8,128)(2,1)} fusion(bf16[448,64]{1,0:T(8,128)(2,1)S(1)} %get-tuple-element.5, bf16[448,64]{1,0:T(8,128)(2,1)S(1)} %get-tuple-element.4), kind=kLoop, calls=%fused_computation.13 | loop fusion | flops 229376 | bytes 229376 | tf_op jit(solution)/shard_map/concatenate | solution.py:24
  12.3 0.3 fusion
  12.7 0.2 compare_reduce_fusion
  12.9 0.4 copy.25
  13.3 0.5 reduce_or.12
  13.8 0.7 %reshape.346.key_pos_ref = s32[4,1,1792]{2,1,0:T(1,128)} reshape(s32[16,448]{1,0:T(8,128)S(1)} %add_add_fusion) | data formatting | bytes 57344 | tf_op jit(solution)/shard_map/reshape | solution.py:334
  14.5 1.8 %fusion.2 = f32[1536,128]{1,0:T(8,128)} fusion(s32[1536]{0:T(1024)S(1)} %add_select_fusion.5, s32[16]{0:T(128)S(1)} %select_reduce_fusion.3, f32[16,64]{1,0:T(8,128)S(1)} %get-tuple-element.17, f32[16,64]{1,0:T(8,128)S(1)} %get-tuple-element.16), kind=kOutput, calls=%fused_computation.9 | convolution fusion | flops 37775360 | bytes 800832 | tf_op jit(solution)/shard_map/dot_general | solution.py:342
  16.3 30.6 %shard_map.95.all_ref = bf16[16,448,256]{2,1,0:T(8,128)(2,1)} custom-call(bf16[448,256]{1,0:T(8,128)(2,1)} %maximum_maximum_fusion.refs_0_), custom_call_target="tpu_custom_call" | custom-call | tf_op jit(solution)/shard_map/pallas_call | solution.py:184
  47.0 14.7 %shard_map.96 = (bf16[56,1024]{1,0:T(8,128)(2,1)}, bf16[96,1024]{1,0:T(8,128)(2,1)}) custom-call(bf16[16,448,256]{2,1,0:T(8,128)(2,1)} %shard_map.95.all_ref, f32[16,96,128]{2,1,0:T(8,128)} %bitcast.10, s32[4,1,1792]{2,1,0:T(1,128)} %reshape.346.key_pos_ref, bf16[448,128]{1,0:T(8,128)(2,1)} %pad_maximum_fusion.query_ref, ...), custom_call_target="tpu_custom_call" | custom-call | tf_op jit(solution)/shard_map/pallas_call | solution.py:305
  (32 shorter events, 0.6 us)
Async XLA Ops:
  0.6 8.9 %copy-start = (bf16[96,1024]{1,0:T(8,128)(2,1)S(1)}, bf16[96,1024]{1,0:T(8,128)(2,1)}, u32[]{:S(2)}) copy-start(bf16[96,1024]{1,0:T(8,128)(2,1)} %param.8) | copy-start | bytes 589828
  7.2 4.1 %copy-start.1 = (bf16[56,1024]{1,0:T(8,128)(2,1)S(1)}, bf16[56,1024]{1,0:T(8,128)(2,1)}, u32[]{:S(2)}) copy-start(bf16[56,1024]{1,0:T(8,128)(2,1)} %param.14) | copy-start | bytes 344068
  9.7 2.6 %copy-start.2 = (s32[16,56]{1,0:T(8,128)S(1)}, s32[16,56]{1,0:T(8,128)}, u32[]{:S(2)}) copy-start(s32[16,56]{1,0:T(8,128)} %param.12) | copy-start | bytes 10756
where the time goes:
time: 62.1 us; the launch traced here: 61.6 us
  Pallas kernels  45.3 us (73%)
  other arithmetic  8.17 us (13%)
  local copies, waits for them, and re-layouts  4.29 us (7%)
  matrix products  3.01 us (5%)
  between operations  0.85 us (1%)
    pallas_call x1, Pallas kernels, spread(): pl.pallas_call(lambda *refs: spread_kernel(count, *refs), out_shape=jax.S...  30.6 us
    pallas_call x1, Pallas kernels, blend(): pl.pallas_call(blend_kernel, grid=(steps,), out_shape=(jax.ShapeDtypeStru...  14.7 us
    dot_general x3, matrix products, pick(): jnp.dot(one_hot.astype(jnp.float32), table, precision=lax.Precision.HIGHEST)  3.01 us
    convert_element_type x1, other arithmetic, shards(): start_angles = passage_start.astype(jnp.float32)[:, None] * frequency  1.37 us

commit v1 on v0

v1 whole, which is shorter than its diff:
```python
import jax
import jax.numpy as jnp
from jax import lax
from jax.experimental import pallas as pl
from jax.experimental.pallas import tpu as pltpu
from jax.sharding import PartitionSpec as P

GROUP = 8
PAGE = 4
ROPE_BASE = 500000.0
LOG2_E = 1.4426950408889634
FAR = 2**30
LOW = -1e30
MESH = pl.DeviceIdType.MESH
FRESH = -1


def pool_parts(rows, count):
    halves = max(2, 2 * (count // 4 - 1))
    half = rows // 2
    cut = max(half, rows * (halves - 1) // halves // 16 * 16)
    lined = [(0, half), (half, cut - half)] if cut > half else [(0, half)]
    return half, lined, (cut, rows - cut)


def iota(shape, dim):
    return lax.broadcasted_iota(jnp.int32, shape, dim)


def divide(number, by):
    return jnp.floor((number.astype(jnp.float32) + 0.5) * (1.0 / by)).astype(jnp.int32)


def total(array, dim):
    return jnp.sum(array, axis=dim, keepdims=True)


def column(row):
    size = row.shape[1]
    same = iota((size, size), 0) == iota((size, size), 1)
    return total(jnp.where(same, jnp.broadcast_to(row, (size, size)), 0), 1)


def split(positions):
    low = positions & 3
    return tuple(
        part.astype(jnp.float32).astype(jnp.bfloat16) for part in (positions - low, low)
    )


def angles(positions, frequency):
    angle = positions.astype(jnp.float32) * frequency
    sine = jnp.sin(angle)
    lower = iota(angle.shape, 1) < angle.shape[1] // 2
    return jnp.cos(angle), jnp.where(lower, -sine, sine)


def turn(vector, cosine, sine):
    return vector * cosine + pltpu.roll(vector, vector.shape[1] // 2, 1) * sine


def dot(left, right):
    return jnp.dot(left, right, preferred_element_type=jnp.float32)


def dot_nt(left, right):
    return lax.dot_general(
        left, right, (((1,), (1,)), ((), ())), preferred_element_type=jnp.float32
    )


def kernel(
    count, pool, *refs,
):
    inputs, refs = refs[:8], refs[8:]
    (attended, pages), refs = refs[:2], refs[2:]
    pool_all, fresh_all, refs = refs[0], refs[1], refs[2:]
    held, refs = refs[:8], refs[8:]
    fresh_kv, fresh_q, slot_ref, order_ref, start_ref, recompute_ref, table_ref, freq_ref = held
    (
        query_ref, limit_ref, cos_ref, sin_ref, key_pos, page_pos, fresh_pos, wanted_ref, keep_ref,
        peak_ref, mixed_ref, page_acc, fresh_acc, send_sem, recv_sem, local_sem,
    ) = refs

    page_count = pool.shape[0]
    tokens = page_count * PAGE
    width = fresh_kv.shape[1]
    dim = width // 2
    sel = fresh_kv.shape[0]
    length = count // 4
    half, lined_pool, last_pool = pool_parts(page_count, count)
    parts = [lined_pool[0], FRESH, *lined_pool[1:], last_pool]
    last = len(parts) - 1
    fresh = 1
    lined = range(last)
    pool_lined = [part for part in lined if part != fresh]
    shared = page_count % count == 0

    me = lax.axis_index("seq")
    at = me // 4
    inner = lax.rem(me, 4)
    core = lax.rem(inner, 2)
    across_inner = lax.rem(inner + 2, 4)
    across = at * 4 + across_inner
    sibling = me + 1 - 2 * core
    twin_inner = inner + 1 - 2 * core
    across_twin = lax.rem(twin_inner + 2, 4)
    up, down = me + 4, me - 4
    has_up, has_down = at < length - 1, at > 0

    barrier = pltpu.get_barrier_semaphore()

    def greet(device):
        pl.semaphore_signal(barrier, inc=1, device_id={"seq": device}, device_id_type=MESH)

    greet(across)
    greet(sibling)
    pl.when(has_up)(lambda: greet(up))
    pl.when(has_down)(lambda: greet(down))

    local = [
        pltpu.make_async_copy(source, target, local_sem.at[at_])
        for at_, (source, target) in enumerate(zip(inputs, held))
    ]
    own_copy = pltpu.make_async_copy(pool, pool_all.at[me], local_sem.at[len(local)])
    for one in local:
        one.start()
    own_copy.start()

    pl.semaphore_wait(barrier, 2 + jnp.where(has_up, 1, 0) + jnp.where(has_down, 1, 0))

    def copy(part, block, way, device, own=False):
        if parts[part] == FRESH:
            source = target = fresh_all.at[block]
        else:
            rows = pl.ds(*parts[part])
            target = pool_all.at[block, rows]
            source = pool.at[rows] if own else target
        return pltpu.make_async_remote_copy(
            src_ref=source,
            dst_ref=target,
            send_sem=send_sem.at[way, part, block],
            recv_sem=recv_sem.at[part, block],
            device_id={"seq": device},
            device_id_type=MESH,
        )

    def begin(part, block, way, device, own=False):
        copy(part, block, way, device, own).start()

    def settle(part, block, way, device, own=False):
        copy(part, block, way, device, own).wait_send()

    def arrive(part, block):
        copy(part, block, 0, sibling).wait_recv()

    def send_lined(act, part):
        pl.when(has_up)(lambda: act(part, me, 0, up, True))
        pl.when(has_down)(lambda: act(part, me, 1, down, True))

    def send_pool(act):
        act(last, me, 2, across, True)
        for part in (*pool_lined, last):
            send_lined(act, part)
        for part in pool_lined:
            act(part, me, 2, across, True)
        for part in (last, *pool_lined):
            act(part, me, 3, sibling, True)

    def send_fresh(act):
        send_lined(act, fresh)
        act(fresh, me, 2, across, True)
        act(fresh, me, 3, sibling, True)

    def pass_across_first(act):
        pl.when(has_up)(lambda: act(last, across, 0, up))
        pl.when(has_down)(lambda: act(last, across, 1, down))
        act(last, across, 3, sibling)

    def line(step, part, act, wait):
        for where in (inner,) if part != last else (inner, across_inner):
            for way, exists, more, device, place in (
                (0, at - step >= 0, has_up, up, at - step),
                (1, at + step < length, has_down, down, at + step),
            ):
                block = place * 4 + where

                @pl.when(exists)
                def _(block=block, way=way, more=more, device=device):
                    if wait:
                        arrive(part, block)
                    pl.when(more)(lambda: act(part, block, way, device))
                    if part != last:
                        act(part, block, 2, across)
                    act(part, block, 3, sibling)

    def crossed(step, part, act, wait):
        for exists, place in (
            (at - step >= 0, at - step),
            ((at + step < length) & (step > 0), at + step),
        ):

            @pl.when(exists)
            def _(place=place):
                block = place * 4 + across_inner
                if wait:
                    arrive(part, block)
                act(part, block, 3, sibling)

    send_pool(begin)

    for one in local:
        one.wait()

    frequency = freq_ref[...]
    lane_mine = iota((1, count), 1) == me
    my_start = total(jnp.where(lane_mine, start_ref[...], 0), 1)
    picked = column(recompute_ref[pl.ds(me, 1), :])
    cosine, sine = angles(my_start + picked, frequency)
    raw = fresh_kv[...]
    turned = turn(raw[:, :dim].astype(jnp.float32), cosine, sine)
    fresh_all[me] = jnp.concatenate(
        [turned, raw[:, dim:].astype(jnp.float32)], axis=1
    ).astype(jnp.bfloat16)

    query_ref[...] = jnp.concatenate(
        [
            turn(fresh_q[:, head * dim : (head + 1) * dim].astype(jnp.float32), cosine, sine)
            for head in range(GROUP)
        ],
        axis=0,
    ).astype(jnp.bfloat16)
    limit_ref[...] = jnp.concatenate([me * tokens + picked] * GROUP, axis=0)
    send_fresh(begin)

    arrive(last, across)
    pass_across_first(begin)

    order = column(order_ref[...])
    slots = total(jnp.where(order == iota((count, count), 1), slot_ref[...], 0), 1)
    square = (count, count)
    slots_row = total(
        jnp.where(iota(square, 0) == iota(square, 1), jnp.broadcast_to(slots, square), 0), 0
    )

    def turn_table(place, block):
        spot = iota((page_count, 1), 0) * count + block
        mine = divide(spot, page_count) == slots_row
        cosine, sine = angles(total(jnp.where(mine, start_ref[...], 0), 1), frequency)
        cos_ref[place] = cosine
        sin_ref[place] = sine

    if shared:
        turn_table(0, 0)
    else:

        @pl.loop(0, count)
        def _(block):
            turn_table(block, block)

    recompute = recompute_ref[...]
    high, low = split(recompute)
    eye = jnp.where(iota((sel, sel), 0) == iota((sel, sel), 1), 1.0, 0.0).astype(jnp.bfloat16)
    high_t = dot_nt(eye, high).astype(jnp.bfloat16)
    low_t = dot_nt(eye, low).astype(jnp.bfloat16)

    def locate(place, first, size):
        lane = iota((1, size), 1)
        token = divide(lane, 4 * half)
        lane = lane - token * (4 * half)
        which = divide(lane, half)
        spot = (lane - which * half + first) * count + place * 4 + which
        slot = divide(spot, page_count)
        page = spot - slot * page_count
        hot = slots == slot
        passage = total(jnp.where(hot, iota((count, size), 0), 0), 0)
        return token, page, passage, hot

    @pl.loop(0, length)
    def _(place):
        for unit in range(2):
            token, page, passage, hot = locate(place, unit * half, PAGE * 4 * half)
            hot = jnp.where(hot, 1.0, 0.0).astype(jnp.bfloat16)
            known = dot(high_t, hot) + dot(low_t, hot)
            spot = page * PAGE + token
            replaced = jnp.max(
                jnp.where(known == spot.astype(jnp.float32), 1, 0), axis=0, keepdims=True
            )
            key_pos[place * 2 + unit] = jnp.where(replaced > 0, FAR, passage * tokens + spot)
            token, page, passage, hot = locate(place, unit * half, 4 * half)
            page_pos[place * 2 + unit] = passage * page_count + page

    many = 4 * sel
    lane = iota((1, many), 1)
    which = divide(lane, sel)
    spread = jnp.where(iota((sel, many), 0) == lane - which * sel, 1.0, 0.0).astype(jnp.bfloat16)
    spread = (dot(high, spread) + dot(low, spread)).astype(jnp.int32)
    spread = spread + iota((count, many), 0) * tokens

    @pl.loop(0, length)
    def _(place):
        chosen = iota((count, many), 0) == place * 4 + which
        fresh_pos[place] = total(jnp.where(chosen, spread, 0), 0)

    row_ids = me * page_count + iota((page_count, 1), 0)
    lanes = table_ref.shape[1]

    def find(at_, wanted):
        match = table_ref[pl.ds(at_, 1), :] == row_ids
        return wanted + jnp.where(match, at_ * lanes + iota((page_count, lanes), 1), 0)

    wanted = lax.fori_loop(
        0, table_ref.shape[0], find, jnp.zeros((page_count, lanes), jnp.int32)
    )
    wanted = total(wanted, 1)
    wanted_ref[...] = wanted
    from_passage = divide(wanted, page_count)
    hot = jnp.where(from_passage == iota((page_count, count), 1), 1.0, 0.0).astype(jnp.bfloat16)
    known = dot(hot, high) + dot(hot, low)
    for token in range(PAGE):
        spot = (wanted - from_passage * page_count) * PAGE + token
        replaced = jnp.max(
            jnp.where(known == spot.astype(jnp.float32), 1.0, 0.0), axis=1, keepdims=True
        )
        keep_ref[token] = 1.0 - replaced

    peak_ref[...] = jnp.full(peak_ref.shape, LOW, jnp.float32)
    mixed_ref[...] = jnp.zeros(mixed_ref.shape, jnp.float32)
    page_acc[...] = jnp.zeros(page_acc.shape, jnp.float32)
    fresh_acc[...] = jnp.zeros(fresh_acc.shape, jnp.float32)
    slope = dim ** (-0.5) * LOG2_E

    def attend(keys, values, positions):
        scores = dot_nt(query_ref[...], keys)
        scores = jnp.where(positions <= limit_ref[...], scores, LOW)
        old_peak = peak_ref[...]
        peak = jnp.maximum(old_peak, jnp.max(scores, axis=1, keepdims=True))
        shrink = jnp.exp2((old_peak - peak) * slope)
        weights = jnp.exp2((scores - peak) * slope).astype(jnp.bfloat16)
        peak_ref[...] = peak
        wide = jnp.concatenate([values, jnp.ones(values.shape, jnp.bfloat16)], axis=1)
        mixed_ref[...] = mixed_ref[...] * shrink + dot(weights, wide)

    def pool_unit(place, unit):
        rows = pl.ds(unit * half, half)
        keys, values = [], []
        for token in range(PAGE):
            for which in range(4):
                block = place * 4 + which
                table = 0 if shared else block
                start = token * width
                raw = pool_all[block, rows, start : start + dim].astype(jnp.float32)
                keys.append(
                    turn(raw, cos_ref[table, rows, :], sin_ref[table, rows, :]).astype(jnp.bfloat16)
                )
                values.append(pool_all[block, rows, start + dim : start + width])
        keys = jnp.concatenate(keys, axis=0)
        values = jnp.concatenate(values, axis=0)
        attend(keys, values, key_pos[place * 2 + unit])
        choose = jnp.where(page_pos[place * 2 + unit] == wanted_ref[...], 1.0, 0.0)
        choose = choose.astype(jnp.bfloat16)
        size = 4 * half
        for token in range(PAGE):
            part = slice(token * size, (token + 1) * size)
            both = jnp.concatenate([keys[part], values[part]], axis=1)
            page_acc[:, token * width : (token + 1) * width] += dot(choose, both)

    def fresh_unit(place):
        both = jnp.concatenate(
            [fresh_all[place * 4 + which].astype(jnp.float32) for which in range(4)], axis=0
        ).astype(jnp.bfloat16)
        positions = fresh_pos[place]
        attend(both[:, :dim], both[:, dim:], positions)
        for token in range(PAGE):
            choose = jnp.where(positions == wanted_ref[...] * PAGE + token, 1.0, 0.0)
            fresh_acc[token] += dot(choose.astype(jnp.bfloat16), both)

    def compute(step, needed, work):
        @pl.loop(0, 2)
        def _(way):
            place = jnp.where(way == 0, at - step, at + step)
            exists = jnp.where(
                way == 0, at - step >= 0, (at + step < length) & (step > 0)
            )

            @pl.when(exists)
            def _():
                for part in needed:
                    arrive(part, place * 4 + twin_inner)
                    arrive(part, place * 4 + across_twin)
                work(place)

    own_copy.wait()

    @pl.loop(0, length)
    def _(step):
        line(step + 1, 0, begin, True)
        crossed(step, 0, begin, True)
        compute(step, (0,), lambda place: pool_unit(place, 0))
        line(step + 1, fresh, begin, True)
        crossed(step, fresh, begin, True)
        compute(step, (fresh,), fresh_unit)
        for part in range(2, last + 1):
            line(step + 1, part, begin, True)
            if part != last:
                crossed(step, part, begin, True)
        compute(step, tuple(range(2, last + 1)), lambda place: pool_unit(place, 1))

    for head in range(GROUP):
        rows = slice(head * sel, (head + 1) * sel)
        attended[:, head * dim : (head + 1) * dim] = (
            mixed_ref[rows, :dim] / mixed_ref[rows, dim:]
        ).astype(jnp.bfloat16)
    for token in range(PAGE):
        columns = slice(token * width, (token + 1) * width)
        pages[:, columns] = jnp.where(
            keep_ref[token] > 0.5, page_acc[:, columns], fresh_acc[token]
        ).astype(jnp.bfloat16)

    send_pool(settle)
    send_fresh(settle)
    pass_across_first(settle)

    @pl.loop(0, length)
    def _(step):
        for part in range(last + 1):
            line(step + 1, part, settle, False)
        for part in lined:
            crossed(step, part, settle, False)


def shards(
    pool_kv, pool_slot, passage_order, passage_start, recompute_pos, page_table, fresh_q, fresh_kv
):
    count = lax.axis_size("seq")
    page_count = pool_kv.shape[0]
    sel, width = fresh_kv.shape
    dim = width // 2
    length = count // 4
    half, lined_pool, _ = pool_parts(page_count, count)
    parts = len(lined_pool) + 2
    tables = 1 if page_count % count == 0 else count
    bf16, f32, i32 = jnp.bfloat16, jnp.float32, jnp.int32
    frequency = ROPE_BASE ** (-(jnp.arange(dim // 2, dtype=f32) * (2.0 / dim)))
    frequency = jnp.concatenate([frequency, frequency])[None, :]
    held = [
        fresh_kv,
        fresh_q,
        pool_slot[None, :],
        passage_order[None, :],
        passage_start[None, :],
        recompute_pos,
        page_table.reshape(-1, 128),
        frequency,
    ]
    queries = sel * GROUP
    return pl.pallas_call(
        lambda *refs: kernel(count, *refs),
        out_shape=(
            jax.ShapeDtypeStruct((sel, GROUP * dim), bf16),
            jax.ShapeDtypeStruct(pool_kv.shape, bf16),
        ),
        in_specs=[pl.BlockSpec(memory_space=pl.ANY)] * (1 + len(held)),
        out_specs=(
            pl.BlockSpec(memory_space=pltpu.VMEM),
            pl.BlockSpec(memory_space=pltpu.VMEM),
        ),
        scratch_shapes=[
            pltpu.VMEM((count, *pool_kv.shape), bf16),
            pltpu.VMEM((count, sel, width), bf16),
            *(pltpu.VMEM(one.shape, one.dtype) for one in held),
            pltpu.VMEM((queries, dim), bf16),
            pltpu.VMEM((queries, 1), i32),
            pltpu.VMEM((tables, page_count, dim), f32),
            pltpu.VMEM((tables, page_count, dim), f32),
            pltpu.VMEM((2 * length, 1, PAGE * 4 * half), i32),
            pltpu.VMEM((2 * length, 1, 4 * half), i32),
            pltpu.VMEM((length, 1, 4 * sel), i32),
            pltpu.VMEM((page_count, 1), i32),
            pltpu.VMEM((PAGE, page_count, 1), f32),
            pltpu.VMEM((queries, 1), f32),
            pltpu.VMEM((queries, width), f32),
            pltpu.VMEM((page_count, PAGE * width), f32),
            pltpu.VMEM((PAGE, page_count, width), f32),
            pltpu.SemaphoreType.DMA((4, parts, count)),
            pltpu.SemaphoreType.DMA((parts, count)),
            pltpu.SemaphoreType.DMA((len(held) + 1,)),
        ],
        compiler_params=pltpu.CompilerParams(collective_id=0, has_side_effects=True),
    )(pool_kv, *held)


def solution(mesh):
    placed = (
        P(("groups", "seq"), None),
        P("groups"),
        P("groups"),
        P("groups"),
        P("groups", None),
        P("groups"),
        P(("groups", "seq"), None),
        P(("groups", "seq"), None),
    )
    return jax.shard_map(
        shards,
        mesh=mesh,
        in_specs=placed,
        out_specs=(P(("groups", "seq"), None), P(("groups", "seq"), None)),
        check_vma=False,
    )
```

time: 62.1 us -> 44 us (0.71)
  other arithmetic: 8.17 us -> 0.6 us
  Pallas kernels: 45.3 us -> 40.3 us
  matrix products: 3.01 us -> 0 us
  local copies, waits for them, and re-layouts: 4.29 us -> 2.27 us
    pallas_call x2 -> x1, Pallas kernels: 45.3 us -> 40.3 us  [shards(): pl.pallas_call(lambda *refs: kernel(count, *refs), out_shape=(jax.ShapeDt...]
    dot_general x3 -> x0, matrix products: 3.01 us -> none  [pick(): jnp.dot(one_hot.astype(jnp.float32), table, precision=lax.Precision.HIGHEST)]
    unnamed x7 -> x4, local copies, waits for them, and re-layouts: 0.06 us -> 2.27 us
    convert_element_type x4 -> x0, other arithmetic: 2.15 us -> none  [the longest x1 1.37 us: shards(): start_angles = passage_start.astype(jnp.float32)[:, None] * frequency]
    reduce_sum x5 -> x0, other arithmetic: 2.12 us -> none  [the longest x1 0.97 us: shards(): jnp.sum(jnp.where(page_table[None, :] == my_rows[:, None], jnp.arange(tot...]
    concatenate x4 -> x0, other arithmetic: 1.73 us -> none  [the longest x2 0.9 us: rotate_pos(): jnp.concatenate([lower_half * cosine - upper_half * sine, upper_half * co...]
    add x6 -> x0, other arithmetic: 1.48 us -> none  [the longest x1 0.78 us: shards(): fresh_place = passage_ids[:, None] * tok_count + recompute_pos]
    reduce_or x2 -> x0, local copies, waits for them, and re-layouts: 0.93 us -> none  [shards(): jnp.any(row_recompute[:, None, :] == row_tok[:, :, None].astype(jnp.float...]
where the time goes in v1:
time: 44 us; the launch traced here: 43.8 us
  Pallas kernels  40.3 us (92%)
  local copies, waits for them, and re-layouts  2.27 us (5%)
  between operations  0.65 us (1%)
  other arithmetic  0.6 us (1%)
    pallas_call x1, Pallas kernels, shards(): pl.pallas_call(lambda *refs: kernel(count, *refs), out_shape=(jax.ShapeDt...  40.3 us
    unnamed x4, local copies, waits for them, and re-layouts  2.27 us

profile of v1, /device:TPU:0, one launch (start us, length us, event | category | flops | bytes accessed | tf_op | source)
XLA Modules:
  0.0 43.8 jit_solution(3897879402074332605)
XLA Ops:
  0.6 0.6 %maximum_bitcast_fusion.refs_8_ = f32[1,128]{1,0:T(1,128)} fusion(f32[64]{0:T(128)S(1)} %negate_power_fusion), kind=kLoop, calls=%fused_computation | loop fusion | flops 128 | bytes 768 | tf_op jit(solution)/shard_map/broadcast_in_dim | solution.py:445
  1.2 40.3 %shard_map.95 = (bf16[56,1024]{1,0:T(8,128)(2,1)}, bf16[96,1024]{1,0:T(8,128)(2,1)}) custom-call(bf16[96,1024]{1,0:T(8,128)(2,1)} %refs_0_.1, bf16[56,256]{1,0:T(8,128)(2,1)} %refs_1_.1, bf16[56,1024]{1,0:T(8,128)(2,1)} %refs_2_.1, s32[1,16]{1,0:T(1,128)} %bitcast.7, s32[1,16]{1,0:T(1,128)} %bitcast.8, s32[1,16]{1,0:T(1,128)} %bitcast.9, s32[16,56]{1,0:T(8,128)} %refs_6_.1, ...), custom_call_target="tpu_custom_call" | custom-call | tf_op jit(solution)/shard_map/pallas_call | solution.py:457
  41.5 0.0 copy-start
  41.5 1.6 %copy.12 = bf16[56,1024]{1,0:T(8,128)(2,1)} copy(bf16[56,1024]{1,0:T(8,128)(2,1)} %get-tuple-element.4) | data formatting | bytes 229376
  43.1 0.0 copy-done
  43.1 0.7 %copy.13 = bf16[96,1024]{1,0:T(8,128)(2,1)} copy(bf16[96,1024]{1,0:T(8,128)(2,1)S(1)} %copy-done) | data formatting | bytes 393216
  (1 shorter events, 0.0 us)
Async XLA Ops:
  41.5 1.6 %copy-start = (bf16[96,1024]{1,0:T(8,128)(2,1)S(1)}, bf16[96,1024]{1,0:T(8,128)(2,1)}, u32[]{:S(2)}) copy-start(bf16[96,1024]{1,0:T(8,128)(2,1)} %get-tuple-element.5) | copy-start | bytes 589828
